TPU v7x, 512 devices: a whole 4x4x16 slice. The times are simulated.
512 devices in a mesh: src: 16 (over z_lo, core), tgt: 32 (over z_hi, y, x).
Axes of the slice: x: 4, y: 4, z: 16 (z_hi: 2, z_lo: 8; z = z_hi * 8 + z_lo), core: 2. Of those that a mesh axis runs over, the one named last changes fastest.
Arguments:
- src_feats: bfloat16 [32, 40960], P(None, ('src', 'tgt')), may hold values from -7 to 7
- src_factor: bfloat16 [16, 40960], P(None, ('src', 'tgt')), may hold values from 0.1 to 8
- tgt_feats: bfloat16 [32, 65536], P(None, ('tgt', 'src')), may hold values from -7 to 7
- tgt_factor: bfloat16 [16, 65536], P(None, ('tgt', 'src')), may hold values from 0.1 to 8
- rank_weight: float32 [16], replicated, may hold values from 0.5 to 4
Outputs:
- grad_src_feats: float32 [32, 40960], P(None, ('src', 'tgt'))
- grad_src_factor: float32 [16, 40960], P(None, ('src', 'tgt'))
- grad_tgt_feats: float32 [32, 65536], P(None, ('tgt', 'src'))
- grad_tgt_factor: float32 [16, 65536], P(None, ('tgt', 'src'))
All inputs are finite; a program needn't handle non-finite values.
Results may differ from a plain program's by a relative error of at most 0.0015.
Values may be sent and summed in bfloat16 or wider, within the bound.
No kernel may reach another device: no remote copies, remote signals or barrier semaphores. Data moves between devices by JAX's collectives and lax.ppermute only.
A program may use at most 64 MiB of HBM per device.

v0:
```python
import jax
import jax.numpy as jnp
from jax import lax
from jax.sharding import PartitionSpec as P


def tile_terms(src_x, src_q, tgt_y, scaled_r, inverse_g):
    sq_src = jnp.sum(jnp.square(src_x.astype(jnp.float32)), 0)
    sq_tgt = jnp.sum(jnp.square(tgt_y.astype(jnp.float32)), 0)
    inner_prod = jnp.dot(src_x.T, tgt_y, preferred_element_type=jnp.float32)
    distance = jnp.sqrt(sq_src[:, None] + sq_tgt[None, :] - 2.0 * inner_prod + 1.0)
    plan_tile = jnp.dot(src_q.T, scaled_r, preferred_element_type=jnp.float32)
    weight = (plan_tile / distance).astype(jnp.bfloat16)
    cost_bf = distance.astype(jnp.bfloat16)
    row_mass = jnp.sum(weight.astype(jnp.float32), 1)
    col_mass = jnp.sum(weight.astype(jnp.float32), 0)
    grad_x = src_x.astype(jnp.float32) * row_mass[None, :] - jnp.dot(
        tgt_y, weight.T, preferred_element_type=jnp.float32
    )
    grad_q = jnp.dot(scaled_r, cost_bf.T, preferred_element_type=jnp.float32)
    grad_y = tgt_y.astype(jnp.float32) * col_mass[None, :] - jnp.dot(
        src_x, weight, preferred_element_type=jnp.float32
    )
    grad_r = inverse_g[:, None] * jnp.dot(src_q, cost_bf, preferred_element_type=jnp.float32)
    return (jnp.concatenate([grad_x, grad_q], 0), jnp.concatenate([grad_y, grad_r], 0))


def block_size(count):
    for candidate in (512, 256, 128):
        return candidate
    return count


def local(src_feats, src_factor, tgt_feats, tgt_factor, rank_weight):
    feature_count = src_feats.shape[0]
    stacked_count = feature_count + src_factor.shape[0]
    inverse_g = 1.0 / rank_weight
    tgt_whole = lax.all_gather(
        jnp.concatenate([tgt_feats, tgt_factor], 0), "src", axis=1, tiled=True
    )
    tgt_points = tgt_whole[:feature_count]
    scaled_r = (tgt_whole[feature_count:].astype(jnp.float32) * inverse_g[:, None]).astype(
        jnp.bfloat16
    )
    col_count = tgt_points.shape[1]
    total_tgt = tgt_feats.shape[1] * lax.axis_size("src") * lax.axis_size("tgt")
    src_stack = jnp.concatenate([src_feats, src_factor], 0)
    src_whole = lax.all_gather(src_stack, "tgt", axis=1, tiled=True)
    row_count = src_whole.shape[1]
    block_rows = block_size(row_count)

    def advance(block_index, totals):
        src_acc, tgt_acc = totals
        offset = block_index * block_rows
        part = lax.dynamic_slice_in_dim(src_whole, offset, block_rows, 1)
        src_part, tgt_part = tile_terms(
            part[:feature_count], part[feature_count:], tgt_points, scaled_r, inverse_g
        )
        src_acc = lax.dynamic_update_slice_in_dim(src_acc, src_part, offset, 1)
        tgt_acc = tgt_acc + tgt_part
        return (src_acc, tgt_acc)

    src_start = jnp.zeros((stacked_count, row_count), jnp.float32)
    tgt_start = jnp.zeros((stacked_count, col_count), jnp.float32)
    src_terms, tgt_terms = lax.fori_loop(
        0, row_count // block_rows, advance, (src_start, tgt_start)
    )
    src_sum = lax.psum_scatter(src_terms, "tgt", scatter_dimension=1, tiled=True)
    tgt_sum = lax.psum_scatter(tgt_terms, "src", scatter_dimension=1, tiled=True)
    scale = 1.0 / total_tgt
    return (
        src_sum[:feature_count] * scale,
        src_sum[feature_count:] * scale,
        tgt_sum[:feature_count] * scale,
        tgt_sum[feature_count:] * scale,
    )


def solution(mesh):
    placed = (
        P(None, ("src", "tgt")),
        P(None, ("src", "tgt")),
        P(None, ("tgt", "src")),
        P(None, ("tgt", "src")),
        P(),
    )
    return jax.shard_map(
        local,
        mesh=mesh,
        in_specs=placed,
        out_specs=(
            P(None, ("src", "tgt")),
            P(None, ("src", "tgt")),
            P(None, ("tgt", "src")),
            P(None, ("tgt", "src")),
        ),
        check_vma=False,
    )
```

profile of v0, /device:TPU:32, one launch (start us, length us, event | category | flops | bytes accessed | tf_op | source)
XLA Modules:
  0.0 646.9 jit_solution(10596549005930550365)
XLA Ops:
  7.2 0.7 broadcast_divide_fusion
  7.9 0.7 pad_maximum_fusion
  8.6 31.1 %all_gather.7 = bf16[48,2048]{1,0:T(8,128)(2,1)S(1)} all-gather(bf16[48,128]{1,0:T(8,128)(2,1)S(1)} %pad_maximum_fusion), channel_id=1, replica_groups=mesh['src'=16,'tgt'=32] {'src'}, dimensions={1}, use_global_device_ids=true | all-gather | bytes 208896 | tf_op jit(solution)/shard_map/all_gather | solution.py:38
  39.8 0.7 maximum_bitcast_fusion
  40.5 160.2 %all-gather = bf16[32,80,48]{1,2,0:T(8,128)(2,1)S(1)} all-gather(bf16[1,80,48]{1,2,0:T(8,128)(2,1)S(1)} %maximum_bitcast_fusion), channel_id=1, replica_groups=mesh['src'=16,'tgt'=32] {'tgt'}, dimensions={0}, use_global_device_ids=true | all-gather | bytes 253440 | tf_op jit(solution)/shard_map/all_gather | solution.py:48
  200.8 0.6 reshape.15
  201.4 29.4 %while.16 = (s32[]{:T(128)}, f32[48,2560]{1,0:T(8,128)S(1)}, f32[48,2048]{1,0:T(8,128)S(1)}, bf16[48,2560]{1,0:T(8,128)(2,1)S(1)}, bf16[16,2048]{1,0:T(8,128)(2,...) while((s32[]{:T(128)}, f32[48,2560]{1,0:T(8,128)S(1)}, ...), condition=%wide.region_5.0_spmd.clone, body=%wide.region_0.0_spmd.clone.sunk | while | flops 314362880 | bytes 25797348 | solution.py:65
  201.5 2.3 add_sqrt_fusion.2
  203.9 0.6 convolution_bitcast_fusion.3
  204.5 0.4 convolution_multiply_fusion.2
  204.9 1.0 convert_reduce_fusion.3
  206.0 0.7 fusion.44
  206.7 0.5 convolution_subtract_fusion.2
  207.4 2.3 add_sqrt_fusion.2
  209.8 0.6 convolution_bitcast_fusion.3
  210.4 0.4 convolution_multiply_fusion.2
  210.8 1.0 convert_reduce_fusion.3
  211.8 0.7 fusion.44
  212.6 0.5 convolution_subtract_fusion.2
  213.3 2.3 add_sqrt_fusion.2
  215.6 0.6 convolution_bitcast_fusion.3
  216.3 0.4 convolution_multiply_fusion.2
  216.7 1.0 convert_reduce_fusion.3
  217.7 0.7 fusion.44
  218.4 0.5 convolution_subtract_fusion.2
  219.2 2.3 add_sqrt_fusion.2
  221.5 0.6 convolution_bitcast_fusion.3
  222.2 0.4 convolution_multiply_fusion.2
  222.6 1.0 convert_reduce_fusion.3
  223.6 0.7 fusion.44
  224.3 0.5 convolution_subtract_fusion.2
  224.8 0.1 maximum_add_fusion.2
  225.1 2.3 add_sqrt_fusion.2
  227.4 0.6 convolution_bitcast_fusion.3
  228.0 0.4 convolution_multiply_fusion.2
  228.5 1.0 convert_reduce_fusion.3
  229.5 0.7 fusion.44
  230.2 0.5 convolution_subtract_fusion.2
  230.9 0.7 copy-done
  231.7 1.5 copy.11
  233.2 88.0 %reduce-scatter.5.cloned.1.call-done = f32[48,128]{1,0:T(8,128)} async-done(((f32[48,2048]{1,0:T(8,128)}), f32[48,128]{1,0:T(8,128)}) %reduce-scatter.5.cloned.1.call-update) | async-done | bytes 24592 | tf_op jit(solution)/shard_map/reduce_scatter | solution.py:69
  321.2 1.3 slice_multiply_fusion.1
  322.5 1.3 slice_multiply_fusion
  323.8 313.2 %reduce-scatter.7.cloned.1.call-done = f32[80,48]{1,0:T(8,128)} async-done(((f32[2560,48]{1,0:T(8,128)}), f32[80,48]{1,0:T(8,128)}) %reduce-scatter.7.cloned.1.call-update) | async-done | bytes 15376
  637.0 0.9 slice.43
  637.9 0.8 copy.13
  638.7 0.6 broadcast_multiply_fusion
  639.4 0.6 broadcast_multiply_fusion.1
  (30 shorter events, 1.4 us)
Async XLA Ops:
  7.2 314.0 %reduce-scatter.5.cloned.1.call-start = ((), (), s32[]{:S(2)}) async-start(), calls=%async_computation.2 | async-start | bytes 417792 | tf_op jit(solution)/shard_map/reduce_scatter | solution.py:69
  230.8 0.8 copy-start
  231.6 405.4 %reduce-scatter.7.cloned.1.call-start = ((), (), s32[]{:S(2)}) async-start(), calls=%async_computation.3 | async-start | bytes 1351680
Sparse Core Ops, SparseCore 0:
  231.7 89.3 reduce-scatter.4
  324.2 312.7 reduce-scatter.6
where the time goes:
time: 647 us
  waiting for transfers between devices  401 us (62%)
  blocking collectives  191 us (30%)
  matrix products  28 us (4%)
  between operations  14.1 us (2%)
  other arithmetic  7.12 us (1%)
    unnamed x3, waiting for transfers between devices  313 us
    all_gather x1, blocking collectives, local(): src_whole = lax.all_gather(src_stack, 'tgt', axis=1, tiled=True)  160 us
    reduce_scatter x1, waiting for transfers between devices, local(): lax.psum_scatter(tgt_terms, 'src', scatter_dimension=1, tiled=True)  88 us
    all_gather x1, blocking collectives, local(): lax.all_gather(jnp.concatenate([tgt_feats, tgt_factor], 0), 'src', axis=1...  31.1 us
  transfers between devices with their start and end apart: 2, of which 2 were waited for; matrix products, arithmetic and copies ran while one was open for 1% of the time, Pallas kernels for 0%

commit v1 on v0

--- a/solution.py
+++ b/solution.py
@@ -1,7 +1,20 @@
+import functools
 import jax
 import jax.numpy as jnp
 from jax import lax
 from jax.sharding import PartitionSpec as P
+
+
+def recover_sources_all(local_values, at_axis):
+    inbox = []
+    for _ in range(lax.axis_size("src")):
+        inbox.append(local_values)
+    even = jnp.stack(inbox, 0)
+    local_part = jnp.concatenate(lax.all_to_all(even, "src", 0, 0), at_axis)
+    return local_part
+
+
+feed_levels_all = functools.partial(recover_sources_all, at_axis=1)
 
 
 def tile_terms(src_x, src_q, tgt_y, scaled_r, inverse_g):
@@ -35,9 +48,7 @@
     feature_count = src_feats.shape[0]
     stacked_count = feature_count + src_factor.shape[0]
     inverse_g = 1.0 / rank_weight
-    tgt_whole = lax.all_gather(
-        jnp.concatenate([tgt_feats, tgt_factor], 0), "src", axis=1, tiled=True
-    )
+    tgt_whole = feed_levels_all(jnp.concatenate([tgt_feats, tgt_factor], 0))
     tgt_points = tgt_whole[:feature_count]
     scaled_r = (tgt_whole[feature_count:].astype(jnp.float32) * inverse_g[:, None]).astype(
         jnp.bfloat16

time: 647 us -> 628 us (0.971)
  blocking collectives: 191 us -> 158 us
  starting transfers between devices: 0.08 us -> 12.7 us
    all_gather x1 -> x0, blocking collectives: 31.1 us -> none  [local(): lax.all_gather(jnp.concatenate([tgt_feats, tgt_factor], 0), 'src', axis=1...]
    all_to_all x0 -> x1, starting transfers between devices: none -> 12.6 us  [recover_sources_all(): local_part = jnp.concatenate(lax.all_to_all(even, 'src', 0, 0), at_axis)]
  transfers between devices with their start and end apart: 2 -> 3, of which waited for: 2 -> 2; matrix products, arithmetic and copies ran while one was open for 1% -> 1% of each run, Pallas kernels for 0% -> 0%
where the time goes in v1:
time: 628 us; the launch traced here: 627 us
  waiting for transfers between devices  401 us (64%)
  blocking collectives  158 us (25%)
  matrix products  28 us (4%)
  between operations  14.1 us (2%)
  starting transfers between devices  12.7 us (2%)
  other arithmetic  7.13 us (1%)
    unnamed x3, waiting for transfers between devices  313 us
    all_gather x1, blocking collectives, local(): src_whole = lax.all_gather(src_stack, 'tgt', axis=1, tiled=True)  158 us
    reduce_scatter x1, waiting for transfers between devices, local(): lax.psum_scatter(tgt_terms, 'src', scatter_dimension=1, tiled=True)  88.5 us
    all_to_all x1, starting transfers between devices, recover_sources_all(): local_part = jnp.concatenate(lax.all_to_all(even, 'src', 0, 0), at_axis)  12.6 us
  transfers between devices with their start and end apart: 3, of which 2 were waited for; matrix products, arithmetic and copies ran while one was open for 1% of the time, Pallas kernels for 0%

profile of v1, /device:TPU:32, one launch (start us, length us, event | category | flops | bytes accessed | tf_op | source)
XLA Modules:
  0.0 627.1 jit_solution(2824988060228032084)
XLA Ops:
  7.2 0.7 pad_maximum_fusion
  7.9 0.7 stack.2
  8.6 12.6 %all-to-all-start = ((bf16[16,48,128]{2,1,0:T(8,128)(2,1)}), bf16[16,48,128]{2,1,0:T(8,128)(2,1)S(1)}, u32[]{:S(2)}, u32[]{:S(2)}) async-start(bf16[16,48,128]{2,1,0:T(8,128)(2,1)} %stack.2), calls=%async_computation | async-start | bytes 393216 | tf_op jit(solution)/shard_map/all_to_all | solution.py:13
  21.3 0.7 maximum_bitcast_fusion
  22.0 158.0 %all-gather = bf16[32,80,48]{1,2,0:T(8,128)(2,1)S(1)} all-gather(bf16[1,80,48]{1,2,0:T(8,128)(2,1)S(1)} %maximum_bitcast_fusion), channel_id=1, replica_groups=mesh['src'=16,'tgt'=32] {'tgt'}, dimensions={0}, use_global_device_ids=true | all-gather | bytes 253440 | tf_op jit(solution)/shard_map/all_gather | solution.py:59
  180.1 0.6 reshape.27
  180.7 0.7 broadcast_divide_fusion
  181.5 29.4 %while.16 = (s32[]{:T(128)}, f32[48,2560]{1,0:T(8,128)S(1)}, f32[48,2048]{1,0:T(8,128)S(1)}, bf16[48,2560]{1,0:T(8,128)(2,1)S(1)}, bf16[16,2048]{1,0:T(8,128)(2,...) while((s32[]{:T(128)}, f32[48,2560]{1,0:T(8,128)S(1)}, ...), condition=%wide.region_5.0_spmd.clone, body=%wide.region_0.0_spmd.clone.sunk | while | flops 314362880 | bytes 25797348 | solution.py:76
  181.6 2.3 add_sqrt_fusion.2
  183.9 0.6 convolution_bitcast_fusion.3
  184.6 0.4 convolution_multiply_fusion.2
  185.0 1.0 convert_reduce_fusion.3
  186.0 0.7 fusion.45
  186.7 0.5 convolution_subtract_fusion.2
  187.5 2.3 add_sqrt_fusion.2
  189.8 0.6 convolution_bitcast_fusion.3
  190.5 0.4 convolution_multiply_fusion.2
  190.9 1.0 convert_reduce_fusion.3
  191.9 0.7 fusion.45
  192.6 0.5 convolution_subtract_fusion.2
  193.4 2.3 add_sqrt_fusion.2
  195.7 0.6 convolution_bitcast_fusion.3
  196.3 0.4 convolution_multiply_fusion.2
  196.7 1.0 convert_reduce_fusion.3
  197.8 0.7 fusion.45
  198.5 0.5 convolution_subtract_fusion.2
  199.2 2.3 add_sqrt_fusion.2
  201.6 0.6 convolution_bitcast_fusion.3
  202.2 0.4 convolution_multiply_fusion.2
  202.6 1.0 convert_reduce_fusion.3
  203.6 0.7 fusion.45
  204.4 0.5 convolution_subtract_fusion.2
  205.1 2.3 add_sqrt_fusion.2
  207.4 0.6 convolution_bitcast_fusion.3
  208.1 0.4 convolution_multiply_fusion.2
  208.5 1.0 convert_reduce_fusion.3
  209.5 0.7 fusion.45
  210.2 0.5 convolution_subtract_fusion.2
  210.9 0.7 copy-done
  211.7 1.5 copy.13
  213.2 88.5 %reduce-scatter.5.cloned.1.call-done = f32[48,128]{1,0:T(8,128)} async-done(((f32[48,2048]{1,0:T(8,128)}), f32[48,128]{1,0:T(8,128)}) %reduce-scatter.5.cloned.1.call-update) | async-done | bytes 24592 | tf_op jit(solution)/shard_map/reduce_scatter | solution.py:80
  301.7 1.3 slice_multiply_fusion.1
  303.0 1.3 slice_multiply_fusion
  304.4 312.9 %reduce-scatter.7.cloned.1.call-done = f32[80,48]{1,0:T(8,128)} async-done(((f32[2560,48]{1,0:T(8,128)}), f32[80,48]{1,0:T(8,128)}) %reduce-scatter.7.cloned.1.call-update) | async-done | bytes 15376
  617.3 0.9 slice.48
  618.1 0.8 copy.15
  619.0 0.6 broadcast_multiply_fusion
  619.7 0.6 broadcast_multiply_fusion.1
  (32 shorter events, 1.5 us)
Async XLA Ops:
  8.6 172.8 %all-to-all-start = ((bf16[16,48,128]{2,1,0:T(8,128)(2,1)}), bf16[16,48,128]{2,1,0:T(8,128)(2,1)S(1)}, u32[]{:S(2)}, u32[]{:S(2)}) async-start(bf16[16,48,128]{2,1,0:T(8,128)(2,1)} %stack.2), calls=%async_computation | async-start | bytes 393216 | tf_op jit(solution)/shard_map/all_to_all | solution.py:13
  21.2 280.5 %reduce-scatter.5.cloned.1.call-start = ((), (), s32[]{:S(2)}) async-start(), calls=%async_computation.3 | async-start | bytes 417792 | tf_op jit(solution)/shard_map/reduce_scatter | solution.py:80
  210.9 0.8 copy-start
  211.7 405.6 %reduce-scatter.7.cloned.1.call-start = ((), (), s32[]{:S(2)}) async-start(), calls=%async_computation.4 | async-start | bytes 1351680
Sparse Core Ops, SparseCore 0:
  211.8 89.8 reduce-scatter.4
  304.8 312.4 reduce-scatter.6
